TPU v7x, 256 devices: a whole 4x4x8 slice. The times are simulated.
256 devices in a mesh: seq: 32 (over z, x), head: 8 (over y, core).
Axes of the slice: x: 4, y: 4, z: 8, core: 2. Of those that a mesh axis runs over, the one named last changes fastest.
Arguments:
- queries: bfloat16 [16384, 1024], P(('seq', 'head')), may hold values from -24 to 24
- keys: bfloat16 [16384, 1024], P(('seq', 'head')), may hold values from -6 to 6
- values: bfloat16 [16384, 1024], P(('seq', 'head')), may hold values from -6 to 6
- out_grad: bfloat16 [16384, 1024], P(('seq', 'head')), may hold values from -6 to 6
- key_blocks: int32 [128, 8], replicated, may hold values from 0 to 127, as said below
- counts: int32 [128], replicated, may hold values from 2 to 8, as said below
Outputs:
- attention: bfloat16 [16384, 1024], P('seq', 'head')
- query_grad: bfloat16 [16384, 1024], P('seq', 'head')
- key_grad: bfloat16 [16384, 1024], P('seq', 'head')
- value_grad: bfloat16 [16384, 1024], P('seq', 'head')
Inputs may be any that keep to these rules, and one draw needn't show every extreme that they name: `counts`: some query block uses all 8 listed blocks. `key_blocks`: row a lists 8 different blocks, the first being block a itself and the second block (a - 1) modulo 128; only the first counts[a] of them are used.
All inputs are finite; a program needn't handle non-finite values.
Results may differ from a plain program's by a relative error of at most 0.015.
Values may be sent and summed in bfloat16 or wider, within the bound.
A program may use at most 64 MiB of HBM per device.

v0:
```python
import math
import jax
import jax.numpy as jnp
from jax import lax
from jax.sharding import PartitionSpec as P

HEADS = 8
BLK = 128
neg_fill = -1e30
tile_limit = 512


def block_table(key_blocks, counts):
    block_count = key_blocks.shape[0]
    slot_ids = jnp.arange(key_blocks.shape[1])
    live_slot = slot_ids[None, :] < counts[:, None]
    matches = (key_blocks[:, :, None] == jnp.arange(block_count)[None, None, :]) & live_slot[
        :, :, None
    ]
    return jnp.any(matches, axis=1).astype(jnp.float32)


def one_hot_rows(first_row, row_total, block_count):
    block_ids = (first_row + jnp.arange(row_total)) // BLK
    return (block_ids[:, None] == jnp.arange(block_count)[None, :]).astype(jnp.float32)


def on_device(queries, keys, values, out_grad, key_blocks, counts):
    heads_here = HEADS // lax.axis_size("head")
    q_rows, k_rows, v_rows, g_rows = (
        lax.all_to_all(queries, "head", split_axis=1, concat_axis=0, tiled=True),
        lax.all_to_all(keys, "head", split_axis=1, concat_axis=0, tiled=True),
        lax.all_to_all(values, "head", split_axis=1, concat_axis=0, tiled=True),
        lax.all_to_all(out_grad, "head", split_axis=1, concat_axis=0, tiled=True),
    )
    row_count = q_rows.shape[0]
    feat_width = q_rows.shape[1]
    head_dim = feat_width // heads_here
    score_scale = 1.0 / math.sqrt(head_dim)
    block_count = key_blocks.shape[0]
    slot_total = key_blocks.shape[1]
    local_blocks = row_count // BLK
    first_block = lax.axis_index("seq") * local_blocks
    listed = lax.dynamic_slice_in_dim(key_blocks, first_block, local_blocks, 0)
    used = lax.dynamic_slice_in_dim(counts, first_block, local_blocks, 0)
    slot_ids = jnp.arange(slot_total)
    live = jnp.repeat(slot_ids[None, :] < used[:, None], BLK, axis=1)
    live_mask = live[:, None, None, :]

    def listed_sets(k_whole, v_whole):
        k_blocks = k_whole.reshape(block_count, BLK, heads_here, head_dim)
        v_blocks = v_whole.reshape(block_count, BLK, heads_here, head_dim)
        key_set = jnp.take(k_blocks, listed, axis=0).reshape(
            local_blocks, slot_total * BLK, heads_here, head_dim
        )
        value_set = jnp.take(v_blocks, listed, axis=0).reshape(
            local_blocks, slot_total * BLK, heads_here, head_dim
        )
        return (key_set, value_set)

    q_blocks = q_rows.reshape(local_blocks, BLK, heads_here, head_dim)
    g_blocks = g_rows.reshape(local_blocks, BLK, heads_here, head_dim)

    def block_scores(key_set):
        scores = (
            jnp.einsum("bqhd,bkhd->bhqk", q_blocks, key_set, preferred_element_type=jnp.float32)
            * score_scale
        )
        return jnp.where(live_mask, scores, neg_fill)

    k_whole, v_whole = (
        lax.all_gather(k_rows, "seq", axis=0, tiled=True),
        lax.all_gather(v_rows, "seq", axis=0, tiled=True),
    )
    key_set, value_set = listed_sets(k_whole, v_whole)
    scores = block_scores(key_set)
    row_max = jnp.max(scores, axis=3)
    weights = jnp.where(live_mask, jnp.exp(scores - row_max[..., None]), 0.0)
    row_sum = jnp.sum(weights, axis=3)
    mixed = jnp.einsum(
        "bhqk,bkhd->bqhd",
        weights.astype(jnp.bfloat16),
        value_set,
        preferred_element_type=jnp.float32,
    )
    attention = (mixed / jnp.transpose(row_sum, (0, 2, 1))[..., None]).astype(jnp.bfloat16)
    block_total = row_max + jnp.log(row_sum)
    block_dot = jnp.sum(g_blocks.astype(jnp.float32) * attention.astype(jnp.float32), axis=3)
    dot_bhq = jnp.transpose(block_dot, (0, 2, 1))
    log_total = jnp.transpose(block_total, (0, 2, 1)).reshape(row_count, heads_here)
    grad_dot = block_dot.reshape(row_count, heads_here)
    k_second, v_second = (
        lax.all_gather(k_rows, "seq", axis=0, tiled=True),
        lax.all_gather(v_rows, "seq", axis=0, tiled=True),
    )
    key_again, value_again = listed_sets(k_second, v_second)
    scores_again = block_scores(key_again)
    probs = jnp.where(live_mask, jnp.exp(scores_again - block_total[..., None]), 0.0)
    dprob = jnp.einsum("bqhd,bkhd->bhqk", g_blocks, value_again, preferred_element_type=jnp.float32)
    dscore = (probs * (dprob - dot_bhq[..., None])).astype(jnp.bfloat16)
    query_acc = jnp.einsum("bhqk,bkhd->bqhd", dscore, key_again, preferred_element_type=jnp.float32)
    all_log_total, all_grad_dot = (
        lax.all_gather(log_total, "seq", axis=0, tiled=True),
        lax.all_gather(grad_dot, "seq", axis=0, tiled=True),
    )
    table = block_table(key_blocks, counts)
    local_hot = one_hot_rows(lax.axis_index("seq") * row_count, row_count, block_count)
    key_table = jnp.einsum("bc,kc->bk", table, local_hot)
    k_heads = k_rows.reshape(row_count, heads_here, head_dim)
    v_heads = v_rows.reshape(row_count, heads_here, head_dim)
    zero_heads = jnp.zeros((row_count, heads_here, head_dim), jnp.float32)
    q_piece = lax.all_gather(q_rows, "seq", axis=0, tiled=True)
    g_piece = lax.all_gather(g_rows, "seq", axis=0, tiled=True)
    piece_rows = q_piece.shape[0]
    tile_rows = math.gcd(piece_rows, tile_limit)

    def tile(tile_index, fold_state):
        offset = tile_index * tile_rows
        q_tile = lax.dynamic_slice_in_dim(q_piece, offset, tile_rows, 0).reshape(
            tile_rows, heads_here, head_dim
        )
        g_tile = lax.dynamic_slice_in_dim(g_piece, offset, tile_rows, 0).reshape(
            tile_rows, heads_here, head_dim
        )
        total_tile = lax.dynamic_slice_in_dim(all_log_total, offset, tile_rows, 0)
        dot_tile = lax.dynamic_slice_in_dim(all_grad_dot, offset, tile_rows, 0)
        query_hot = one_hot_rows(offset, tile_rows, block_count)
        allowed = jnp.einsum("qb,bk->qk", query_hot, key_table) > 0.5
        tile_scores = (
            jnp.einsum("qhd,khd->qhk", q_tile, k_heads, preferred_element_type=jnp.float32)
            * score_scale
        )
        tile_scores = jnp.where(allowed[:, None, :], tile_scores, neg_fill)
        tile_probs = jnp.where(
            allowed[:, None, :], jnp.exp(tile_scores - total_tile[:, :, None]), 0.0
        )
        value_acc = fold_state[1] + jnp.einsum(
            "qhk,qhd->khd",
            tile_probs.astype(jnp.bfloat16),
            g_tile,
            preferred_element_type=jnp.float32,
        )
        tile_dprob = jnp.einsum("qhd,khd->qhk", g_tile, v_heads, preferred_element_type=jnp.float32)
        tile_ds = (tile_probs * (tile_dprob - dot_tile[:, :, None])).astype(jnp.bfloat16)
        key_acc = fold_state[0] + jnp.einsum(
            "qhk,qhd->khd", tile_ds, q_tile, preferred_element_type=jnp.float32
        )
        return (key_acc, value_acc)

    key_acc, value_acc = lax.fori_loop(0, piece_rows // tile_rows, tile, (zero_heads, zero_heads))
    query_grad = (query_acc * score_scale).astype(jnp.bfloat16).reshape(row_count, feat_width)
    key_grad = (key_acc * score_scale).astype(jnp.bfloat16).reshape(row_count, feat_width)
    value_grad = value_acc.astype(jnp.bfloat16).reshape(row_count, feat_width)
    return (attention.reshape(row_count, feat_width), query_grad, key_grad, value_grad)


def solution(mesh):
    in_specs = (
        P(("seq", "head"), None),
        P(("seq", "head"), None),
        P(("seq", "head"), None),
        P(("seq", "head"), None),
        P(),
        P(),
    )
    out_specs = (P("seq", "head"), P("seq", "head"), P("seq", "head"), P("seq", "head"))
    return jax.shard_map(
        on_device, mesh=mesh, in_specs=in_specs, out_specs=out_specs, check_vma=False
    )
```

profile of v0, /device:TPU:8, one launch (start us, length us, event | category | flops | bytes accessed | tf_op | source)
XLA Modules:
  0.0 496.2 jit_solution(53246647357267488)
XLA Ops:
  8.1 9.9 %all_to_all.76 = bf16[64,8,128]{2,0,1:T(8,128)(2,1)} all-to-all(bf16[64,8,128]{2,0,1:T(8,128)(2,1)S(1)} %copy_bitcast_fusion.2), channel_id=1, replica_groups=mesh['seq'=32,'head'=8] {'head'}, dimensions={1} | all-to-all | bytes 262144 | tf_op jit(solution)/shard_map/all_to_all | solution.py:32
  19.0 9.2 %all_to_all.77 = bf16[64,8,128]{2,0,1:T(8,128)(2,1)} all-to-all(bf16[64,8,128]{2,0,1:T(8,128)(2,1)S(1)} %copy_bitcast_fusion.3), channel_id=1, replica_groups=mesh['seq'=32,'head'=8] {'head'}, dimensions={1} | all-to-all | bytes 262144 | tf_op jit(solution)/shard_map/all_to_all | solution.py:33
  29.1 9.2 %all_to_all.78 = bf16[64,8,128]{2,0,1:T(8,128)(2,1)} all-to-all(bf16[64,8,128]{2,0,1:T(8,128)(2,1)S(1)} %copy_bitcast_fusion.1), channel_id=1, replica_groups=mesh['seq'=32,'head'=8] {'head'}, dimensions={1} | all-to-all | bytes 262144 | tf_op jit(solution)/shard_map/all_to_all | solution.py:31
  39.3 9.2 %all_to_all.79 = bf16[64,8,128]{2,0,1:T(8,128)(2,1)} all-to-all(bf16[64,8,128]{2,0,1:T(8,128)(2,1)S(1)} %copy_bitcast_fusion), channel_id=1, replica_groups=mesh['seq'=32,'head'=8] {'head'}, dimensions={1} | all-to-all | bytes 262144 | tf_op jit(solution)/shard_map/all_to_all | solution.py:34
  50.0 51.3 %all-gather.7.cloned.1.call-done = bf16[16384,128]{1,0:T(8,128)(2,1)} async-done(((bf16[512,128]{1,0:T(8,128)(2,1)}), bf16[16384,128]{1,0:T(8,128)(2,1)}) %all-gather.7.cloned.1.call-update) | async-done | bytes 4194320 | tf_op jit(solution)/shard_map/all_gather | solution.py:72
  101.3 2.9 gather_fusion.1
  104.3 78.2 %all-gather.5.cloned.1.call-done = bf16[16384,128]{1,0:T(8,128)(2,1)} async-done(((bf16[512,128]{1,0:T(8,128)(2,1)}), bf16[16384,128]{1,0:T(8,128)(2,1)}) %all-gather.5.cloned.1.call-update) | async-done | bytes 4194320 | tf_op jit(solution)/shard_map/all_gather | solution.py:73
  182.5 2.9 gather_fusion
  188.5 47.6 %all_gather.23 = f32[16384,1]{0,1:T(1,128)S(1)} all-gather(f32[512,1]{0,1:T(1,128)S(1)} %bitcast.245), channel_id=1, replica_groups=mesh['seq'=32,'head'=8] {'seq'}, dimensions={0}, use_global_device_ids=true | all-gather | bytes 67584 | tf_op jit(solution)/shard_map/all_gather | solution.py:103
  236.1 2.7 fusion.54
  238.8 47.4 %all_gather.25 = f32[16384,1]{0,1:T(1,128)S(1)} all-gather(f32[512,1]{0,1:T(1,128)S(1)} %bitcast.246), channel_id=1, replica_groups=mesh['seq'=32,'head'=8] {'seq'}, dimensions={0}, use_global_device_ids=true | all-gather | bytes 67584 | tf_op jit(solution)/shard_map/all_gather | solution.py:104
  286.1 3.5 fusion.41
  289.6 55.2 %all-gather.11.cloned.1.call-done = bf16[16384,128]{1,0:T(8,128)(2,1)} async-done(((bf16[512,128]{1,0:T(8,128)(2,1)}), bf16[16384,128]{1,0:T(8,128)(2,1)}) %all-gather.11.cloned.1.call-update) | async-done | bytes 4194320 | tf_op jit(solution)/shard_map/all_gather | solution.py:113
  344.8 143.3 %while.18 = (s32[]{:T(128)}, f32[512,1,128]{0,2,1:T(8,128)S(1)}, f32[512,1,128]{0,2,1:T(8,128)S(1)}, bf16[16384,128]{1,0:T(8,128)(2,1)}, bf16[128,512]{1,0:T(8,1...) while((s32[]{:T(128)}, f32[512,1,128]{0,2,1:T(8,128)S(1)}, ...), condition=%wide.region_5.7_spmd.clone, body=%wide.region_4.6_spmd.clone.sunk | while | flops 338239488 | bytes 5654229 | solution.py:150
  346.6 1.5 fusion.97
  355.5 1.5 fusion.97
  360.0 1.5 fusion.97
  369.0 1.5 fusion.97
  373.5 1.5 fusion.97
  382.4 1.5 fusion.97
  395.8 1.5 fusion.97
  409.3 1.5 fusion.97
  422.7 1.5 fusion.97
  427.2 1.5 fusion.97
  436.1 1.5 fusion.97
  440.6 1.5 fusion.97
  449.6 1.5 fusion.97
  454.0 1.5 fusion.97
  463.0 1.5 fusion.97
  467.5 1.5 fusion.97
  476.4 1.5 fusion.97
  480.9 1.5 fusion.97
  (228 shorter events, 124.0 us)
Async XLA Ops:
  7.2 0.9 copy-start
  7.2 41.3 %copy-start.7 = (s32[128,8]{0,1:T(8,128)S(1)}, s32[128,8]{0,1:T(8,128)}, u32[]{:S(2)}) copy-start(s32[128,8]{0,1:T(8,128)} %param.14) | copy-start | bytes 12292
  7.2 41.8 %copy-start.8 = (s32[128]{0:T(128)S(1)}, s32[128]{0:T(128)}, u32[]{:S(2)}) copy-start(s32[128]{0:T(128)} %param.15) | copy-start | bytes 1540
  7.2 94.1 %all-gather.7.cloned.1.call-start = ((), (), s32[]{:S(2)}) async-start(), calls=%async_computation.5 | async-start | bytes 4325376 | tf_op jit(solution)/shard_map/all_gather | solution.py:72
  18.0 164.5 %all-gather.5.cloned.1.call-start = ((), (), s32[]{:S(2)}) async-start(), calls=%async_computation.4 | async-start | bytes 4325376 | tf_op jit(solution)/shard_map/all_gather | solution.py:73
  28.2 261.5 %all-gather.9.cloned.1.call-start = ((), (), s32[]{:S(2)}) async-start(), calls=%async_computation.6 | async-start | bytes 4325376 | tf_op jit(solution)/shard_map/all_gather | solution.py:112
  38.3 306.5 %all-gather.11.cloned.1.call-start = ((), (), s32[]{:S(2)}) async-start(), calls=%async_computation.7 | async-start | bytes 4325376 | tf_op jit(solution)/shard_map/all_gather | solution.py:113
  185.4 0.9 copy-start.5
  185.7 2.7 copy-start.2
  185.7 50.3 %copy-start.3 = (bf16[4,8,128,1,128]{4,2,1,0,3:T(8,128)(2,1)}, bf16[4,8,128,1,128]{4,2,1,0,3:T(8,128)(2,1)S(1)}, u32[]{:S(2)}) copy-start(bf16[4,8,128,1,128]{4,2,1,0,3:T(8,128)(2,1)S(1)} %get-tuple-element.309) | copy-start | bytes 3145732
  186.3 49.7 %copy-start.6 = (bf16[64,8,128]{2,0,1:T(8,128)(2,1)S(1)}, bf16[64,8,128]{2,0,1:T(8,128)(2,1)}, u32[]{:S(2)}) copy-start(bf16[64,8,128]{2,0,1:T(8,128)(2,1)} %all_to_all.79) | copy-start | bytes 393220
  286.1 58.7 %copy-start.1 = (bf16[64,8,128]{2,0,1:T(8,128)(2,1)S(1)}, bf16[64,8,128]{2,0,1:T(8,128)(2,1)}, u32[]{:S(2)}) copy-start(bf16[64,8,128]{2,0,1:T(8,128)(2,1)} %all_to_all.77) | copy-start | bytes 393220
  286.1 58.7 %copy-start.4 = (bf16[64,8,128]{2,0,1:T(8,128)(2,1)S(1)}, bf16[64,8,128]{2,0,1:T(8,128)(2,1)}, u32[]{:S(2)}) copy-start(bf16[64,8,128]{2,0,1:T(8,128)(2,1)} %all_to_all.76) | copy-start | bytes 393220
Sparse Core Ops, SparseCore 0:
  18.1 83.1 all-gather.6
  103.9 78.5 all-gather.4
  185.1 78.5 all-gather.8
  266.1 78.6 all-gather.10
where the time goes:
time: 498 us; the launch traced here: 496 us
  waiting for transfers between devices  185 us (37%)
  matrix products  148 us (30%)
  blocking collectives  132 us (27%)
  between operations  14 us (3%)
  local copies, waits for them, and re-layouts  11.9 us (2%)
    all_gather x1, waiting for transfers between devices, on_device(): lax.all_gather(v_rows, 'seq', axis=0, tiled=True)  78.2 us
    all_gather x1, waiting for transfers between devices, on_device(): g_piece = lax.all_gather(g_rows, 'seq', axis=0, tiled=True)  55.2 us
    all_gather x1, waiting for transfers between devices, on_device(): lax.all_gather(k_rows, 'seq', axis=0, tiled=True)  51.3 us
    dot_general x32, matrix products, tile(): jnp.einsum('qhk,qhd->khd', tile_ds, q_tile, preferred_element_type=jnp.fl...  47.7 us
    all_gather x1, blocking collectives, on_device(): lax.all_gather(log_total, 'seq', axis=0, tiled=True)  47.6 us
    all_gather x1, blocking collectives, on_device(): lax.all_gather(grad_dot, 'seq', axis=0, tiled=True)  47.4 us
    dot_general x32, matrix products, tile(): jnp.einsum('qhd,khd->qhk', q_tile, k_heads, preferred_element_type=jnp.fl...  43.6 us
    dot_general x32, matrix products, tile(): jnp.einsum('qhk,qhd->khd', tile_probs.astype(jnp.bfloat16), g_tile, prefe...  37.8 us
  transfers between devices with their start and end apart: 4, of which 3 were waited for; matrix products, arithmetic and copies ran while one was open for 4% of the time, Pallas kernels for 0%

commit v1 on v0

--- a/solution.py
+++ b/solution.py
@@ -69,7 +69,9 @@
         return jnp.where(live_mask, scores, neg_fill)
 
     k_whole, v_whole = (
-        lax.all_gather(k_rows, "seq", axis=0, tiled=True),
+        jnp.concatenate(
+            lax.all_to_all(jnp.stack([k_rows] * lax.axis_size("seq")), "seq", 0, 0), axis=0
+        ),
         lax.all_gather(v_rows, "seq", axis=0, tiled=True),
     )
     key_set, value_set = listed_sets(k_whole, v_whole)

time: 498 us -> 583 us (1.17)
  matrix products: 148 us -> 181 us
  waiting for transfers between devices: 185 us -> 216 us
  starting transfers between devices: 0.16 us -> 11.3 us
  local copies, waits for them, and re-layouts: 11.9 us -> 19.7 us
    all_to_all x0 -> x1, waiting for transfers between devices: none -> 32 us  [on_device(): lax.all_to_all(jnp.stack([k_rows] * lax.axis_size('seq')), 'seq', 0, 0)]
    all_gather x1, waiting for transfers between devices: 51.3 us -> 79.1 us  [on_device(): lax.all_gather(k_rows, 'seq', axis=0, tiled=True)]
    all_gather x1, waiting for transfers between devices: 78.2 us -> 50.5 us  [on_device(): lax.all_gather(v_rows, 'seq', axis=0, tiled=True)]
    dot_general x32, matrix products: 11.2 us -> 33.8 us  [tile(): allowed = jnp.einsum('qb,bk->qk', query_hot, key_table) > 0.5]
    all_to_all x0 -> x1, starting transfers between devices: none -> 11.2 us  [on_device(): lax.all_to_all(jnp.stack([k_rows] * lax.axis_size('seq')), 'seq', 0, 0)]
    dot_general x32, matrix products: 43.6 us -> 51.1 us  [tile(): jnp.einsum('qhd,khd->qhk', q_tile, k_heads, preferred_element_type=jnp.fl...]
  transfers between devices with their start and end apart: 4 -> 5, of which waited for: 3 -> 4; matrix products, arithmetic and copies ran while one was open for 4% -> 5% of each run, Pallas kernels for 0% -> 0%
where the time goes in v1:
time: 583 us; the launch traced here: 581 us
  waiting for transfers between devices  216 us (37%)
  matrix products  181 us (31%)
  blocking collectives  132 us (23%)
  local copies, waits for them, and re-layouts  19.7 us (3%)
  between operations  13.9 us (2%)
  starting transfers between devices  11.3 us (2%)
    all_gather x1, waiting for transfers between devices, on_device(): lax.all_gather(k_rows, 'seq', axis=0, tiled=True)  79.1 us
    all_gather x1, waiting for transfers between devices, on_device(): g_piece = lax.all_gather(g_rows, 'seq', axis=0, tiled=True)  53.3 us
    dot_general x32, matrix products, tile(): jnp.einsum('qhd,khd->qhk', q_tile, k_heads, preferred_element_type=jnp.fl...  51.1 us
    all_gather x1, waiting for transfers between devices, on_device(): lax.all_gather(v_rows, 'seq', axis=0, tiled=True)  50.5 us
    all_gather x1, blocking collectives, on_device(): lax.all_gather(log_total, 'seq', axis=0, tiled=True)  47.8 us
    dot_general x32, matrix products, tile(): jnp.einsum('qhk,qhd->khd', tile_ds, q_tile, preferred_element_type=jnp.fl...  47.7 us
    all_gather x1, blocking collectives, on_device(): lax.all_gather(grad_dot, 'seq', axis=0, tiled=True)  47.3 us
    dot_general x32, matrix products, tile(): jnp.einsum('qhk,qhd->khd', tile_probs.astype(jnp.bfloat16), g_tile, prefe...  37.8 us
  transfers between devices with their start and end apart: 5, of which 4 were waited for; matrix products, arithmetic and copies ran while one was open for 5% of the time, Pallas kernels for 0%

profile of v1, /device:TPU:8, one launch (start us, length us, event | category | flops | bytes accessed | tf_op | source)
XLA Modules:
  0.0 580.8 jit_solution(9745322151400641127)
XLA Ops:
  8.1 9.9 %all_to_all.78 = bf16[64,8,128]{2,0,1:T(8,128)(2,1)} all-to-all(bf16[64,8,128]{2,0,1:T(8,128)(2,1)S(1)} %copy_bitcast_fusion.2), channel_id=1, replica_groups=mesh['seq'=32,'head'=8] {'head'}, dimensions={1} | all-to-all | bytes 262144 | tf_op jit(solution)/shard_map/all_to_all | solution.py:32
  19.0 9.2 %all_to_all.79 = bf16[64,8,128]{2,0,1:T(8,128)(2,1)} all-to-all(bf16[64,8,128]{2,0,1:T(8,128)(2,1)S(1)} %copy_bitcast_fusion.3), channel_id=1, replica_groups=mesh['seq'=32,'head'=8] {'head'}, dimensions={1} | all-to-all | bytes 262144 | tf_op jit(solution)/shard_map/all_to_all | solution.py:33
  29.1 9.2 %all_to_all.80 = bf16[64,8,128]{2,0,1:T(8,128)(2,1)} all-to-all(bf16[64,8,128]{2,0,1:T(8,128)(2,1)S(1)} %copy_bitcast_fusion.1), channel_id=1, replica_groups=mesh['seq'=32,'head'=8] {'head'}, dimensions={1} | all-to-all | bytes 262144 | tf_op jit(solution)/shard_map/all_to_all | solution.py:31
  39.3 9.2 %all_to_all.81 = bf16[64,8,128]{2,0,1:T(8,128)(2,1)} all-to-all(bf16[64,8,128]{2,0,1:T(8,128)(2,1)S(1)} %copy_bitcast_fusion), channel_id=1, replica_groups=mesh['seq'=32,'head'=8] {'head'}, dimensions={1} | all-to-all | bytes 262144 | tf_op jit(solution)/shard_map/all_to_all | solution.py:34
  48.4 3.8 stack.5
  52.3 11.2 %all-to-all-start.2 = ((bf16[32,512,128]{2,1,0:T(8,128)(2,1)}), bf16[32,512,128]{2,1,0:T(8,128)(2,1)}, u32[]{:S(2)}, u32[]{:S(2)}) async-start(bf16[32,512,128]{2,1,0:T(8,128)(2,1)} %stack.5), calls=%async_computation.2 | async-start | bytes 8388608 | tf_op jit(solution)/shard_map/all_to_all | solution.py:73
  65.6 79.1 %all-gather.7.cloned.1.call-done = bf16[16384,128]{1,0:T(8,128)(2,1)} async-done(((bf16[512,128]{1,0:T(8,128)(2,1)}), bf16[16384,128]{1,0:T(8,128)(2,1)}) %all-gather.7.cloned.1.call-update) | async-done | bytes 4194320 | tf_op jit(solution)/shard_map/all_gather | solution.py:95
  144.7 2.9 gather_fusion.2
  147.6 32.0 %all-to-all-done.2 = bf16[32,512,128]{2,1,0:T(8,128)(2,1)} async-done(((bf16[32,512,128]{2,1,0:T(8,128)(2,1)}), bf16[32,512,128]{2,1,0:T(8,128)(2,1)}, u32[]{:S(2)}, u32[]{:S(2)}) %all-to-all-start.2) | async-done | bytes 4194336 | tf_op jit(solution)/shard_map/all_to_all | solution.py:73
  179.6 3.9 gather_fusion.1
  183.5 50.5 %all-gather.5.cloned.1.call-done = bf16[16384,128]{1,0:T(8,128)(2,1)} async-done(((bf16[512,128]{1,0:T(8,128)(2,1)}), bf16[16384,128]{1,0:T(8,128)(2,1)}) %all-gather.5.cloned.1.call-update) | async-done | bytes 4194320 | tf_op jit(solution)/shard_map/all_gather | solution.py:75
  234.1 3.8 gather_fusion
  237.9 1.9 broadcast_select_fusion
  242.6 47.8 %all_gather.22 = f32[16384,1]{0,1:T(1,128)S(1)} all-gather(f32[512,1]{0,1:T(1,128)S(1)} %bitcast.233), channel_id=1, replica_groups=mesh['seq'=32,'head'=8] {'seq'}, dimensions={0}, use_global_device_ids=true | all-gather | bytes 67584 | tf_op jit(solution)/shard_map/all_gather | solution.py:105
  290.3 3.6 fusion.56
  293.9 47.3 %all_gather.24 = f32[16384,1]{0,1:T(1,128)S(1)} all-gather(f32[512,1]{0,1:T(1,128)S(1)} %bitcast.234), channel_id=1, replica_groups=mesh['seq'=32,'head'=8] {'seq'}, dimensions={0}, use_global_device_ids=true | all-gather | bytes 67584 | tf_op jit(solution)/shard_map/all_gather | solution.py:106
  341.2 1.8 fusion.69
  343.0 53.3 %all-gather.11.cloned.1.call-done = bf16[16384,128]{1,0:T(8,128)(2,1)} async-done(((bf16[512,128]{1,0:T(8,128)(2,1)}), bf16[16384,128]{1,0:T(8,128)(2,1)}) %all-gather.11.cloned.1.call-update) | async-done | bytes 4194320 | tf_op jit(solution)/shard_map/all_gather | solution.py:115
  396.3 172.4 %while.18 = (s32[]{:T(128)}, f32[512,1,128]{0,2,1:T(8,128)S(1)}, f32[512,1,128]{0,2,1:T(8,128)S(1)}, bf16[16384,128]{1,0:T(8,128)(2,1)}, bf16[128,512]{1,0:T(8,1...) while((s32[]{:T(128)}, f32[512,1,128]{0,2,1:T(8,128)S(1)}, ...), condition=%wide.region_5.7_spmd.clone, body=%wide.region_4.6_spmd.clone.sunk | while | flops 338239488 | bytes 5654229 | solution.py:152
  397.4 1.6 fusion.105
  402.8 1.6 fusion.105
  418.9 1.6 fusion.105
  435.1 1.6 fusion.105
  451.3 1.6 fusion.105
  467.4 1.6 fusion.105
  483.6 1.6 fusion.105
  489.0 1.6 fusion.105
  499.8 1.6 fusion.105
  505.2 1.6 fusion.105
  521.3 1.6 fusion.105
  537.5 1.6 fusion.105
  570.3 3.9 fusion.38
  (231 shorter events, 161.8 us)
Async XLA Ops:
  7.2 0.9 copy-start
  7.2 137.5 %all-gather.7.cloned.1.call-start = ((), (), s32[]{:S(2)}) async-start(), calls=%async_computation.6 | async-start | bytes 4325376 | tf_op jit(solution)/shard_map/all_gather | solution.py:95
  18.0 216.1 %all-gather.5.cloned.1.call-start = ((), (), s32[]{:S(2)}) async-start(), calls=%async_computation.5 | async-start | bytes 4325376 | tf_op jit(solution)/shard_map/all_gather | solution.py:75
  28.2 314.9 %all-gather.9.cloned.1.call-start = ((), (), s32[]{:S(2)}) async-start(), calls=%async_computation.7 | async-start | bytes 4325376 | tf_op jit(solution)/shard_map/all_gather | solution.py:114
  52.3 11.8 %copy-start.7 = (s32[128]{0:T(128)S(1)}, s32[128]{0:T(128)}, u32[]{:S(2)}) copy-start(s32[128]{0:T(128)} %param.15) | copy-start | bytes 1540
  52.3 12.1 %copy-start.6 = (s32[128,8]{0,1:T(8,128)S(1)}, s32[128,8]{0,1:T(8,128)}, u32[]{:S(2)}) copy-start(s32[128,8]{0,1:T(8,128)} %param.14) | copy-start | bytes 12292
  52.3 127.4 %all-to-all-start.2 = ((bf16[32,512,128]{2,1,0:T(8,128)(2,1)}), bf16[32,512,128]{2,1,0:T(8,128)(2,1)}, u32[]{:S(2)}, u32[]{:S(2)}) async-start(bf16[32,512,128]{2,1,0:T(8,128)(2,1)} %stack.5), calls=%async_computation.2 | async-start | bytes 8388608 | tf_op jit(solution)/shard_map/all_to_all | solution.py:73
  63.5 332.9 %all-gather.11.cloned.1.call-start = ((), (), s32[]{:S(2)}) async-start(), calls=%async_computation.8 | async-start | bytes 4325376 | tf_op jit(solution)/shard_map/all_gather | solution.py:115
  237.9 1.9 copy-start.3
  239.8 50.5 %copy-start.4 = (bf16[4,8,128,1,128]{4,2,1,0,3:T(8,128)(2,1)}, bf16[4,8,128,1,128]{4,2,1,0,3:T(8,128)(2,1)S(1)}, u32[]{:S(2)}) copy-start(bf16[4,8,128,1,128]{4,2,1,0,3:T(8,128)(2,1)S(1)} %get-tuple-element.310) | copy-start | bytes 3145732
  239.8 50.5 %copy-start.5 = (bf16[64,8,128]{2,0,1:T(8,128)(2,1)S(1)}, bf16[64,8,128]{2,0,1:T(8,128)(2,1)}, u32[]{:S(2)}) copy-start(bf16[64,8,128]{2,0,1:T(8,128)(2,1)} %all_to_all.81) | copy-start | bytes 393220
  293.9 102.4 %copy-start.1 = (bf16[64,8,128]{2,0,1:T(8,128)(2,1)S(1)}, bf16[64,8,128]{2,0,1:T(8,128)(2,1)}, u32[]{:S(2)}) copy-start(bf16[64,8,128]{2,0,1:T(8,128)(2,1)} %all_to_all.79) | copy-start | bytes 393220
  293.9 102.4 %copy-start.2 = (bf16[64,8,128]{2,0,1:T(8,128)(2,1)S(1)}, bf16[64,8,128]{2,0,1:T(8,128)(2,1)}, u32[]{:S(2)}) copy-start(bf16[64,8,128]{2,0,1:T(8,128)(2,1)} %all_to_all.78) | copy-start | bytes 393220
Sparse Core Ops, SparseCore 0:
  18.1 126.5 all-gather.6
  147.3 86.7 all-gather.4
  236.6 78.5 all-gather.8
  317.7 78.5 all-gather.10
